TPU v7x, 512 devices: a whole 4x8x8 slice. The times are simulated.
512 devices in a mesh: aux: 8 (over z), ao: 16 (over y, core), orb: 4 (over x).
Axes of the slice: x: 4, y: 8, z: 8, core: 2. Of those that a mesh axis runs over, the one named last changes fastest.
Arguments:
- integrals: bfloat16 [128, 16, 4, 128, 128], P('aux', 'ao', None, 'orb'), may hold values from -6 to 6
- partner: int32 [16, 4], P('ao'), may hold values from 0 to 15
- pair_count: int32 [16], P('ao'), may hold values from 1 to 4
- occupied_coeff: bfloat16 [2048, 512], P('ao', 'orb'), may hold values from -0.25 to 0.25
- occupied_domain: int32 [16, 4], P('ao', 'orb'), may hold values 0 or 1
- virtual_coeff: bfloat16 [2048, 8192], P('aux', 'ao'), may hold values from -0.125 to 0.125
- virtual_domain: int32 [16, 64], P(None, 'ao'), may hold values 0 or 1
Outputs:
- transformed: bfloat16 [128, 512, 8192], P('aux', 'orb', 'ao')
All inputs are finite; a program needn't handle non-finite values. No bound on the sum of `occupied_domain` or of `virtual_domain` on one device may be relied on, other than what follows from the above.
Results may differ from a plain program's by a relative error of at most 0.0049.
Values may be sent and summed in bfloat16 or wider, within the bound.
A program may use at most 64 MiB of HBM per device.

v0:
```python
import jax
import jax.numpy as jnp
from jax import lax
from jax.sharding import PartitionSpec as P


def local(
    integrals, partner, pair_count, occupied_coeff, occupied_domain, virtual_coeff, virtual_domain
):
    block_size = integrals.shape[4]
    slab_rows = integrals.shape[0]
    slot_count = integrals.shape[2]
    occ_width = occupied_coeff.shape[1]
    occ_local = occupied_coeff * occupied_domain.astype(jnp.bfloat16)
    all_occ = lax.all_gather(occ_local, "ao", axis=0, tiled=True)
    all_ints = lax.all_gather(integrals, "orb", axis=3, tiled=True)
    vir_blocks = virtual_coeff.shape[0] // block_size
    first = lax.axis_index("aux") * vir_blocks
    dom = lax.dynamic_slice_in_dim(virtual_domain, first, vir_blocks, axis=0).astype(jnp.bfloat16)
    dom = jnp.repeat(jnp.repeat(dom, block_size, axis=0), block_size, axis=1)
    vir_masked = lax.all_gather(virtual_coeff * dom, "aux", axis=0, tiled=True)
    picked = all_occ.reshape(-1, block_size, occ_width)[partner[0]]
    slots = jnp.arange(slot_count, dtype=jnp.int32)
    live = (slots < pair_count[0]).astype(jnp.bfloat16)
    picked = picked * live[:, None, None]
    half = jnp.einsum(
        "kri,pkrv->piv", picked, all_ints[:, 0], preferred_element_type=jnp.float32
    ).astype(jnp.bfloat16)
    piece = lax.all_gather(half, "ao", axis=2, tiled=True)
    flat = piece.reshape(slab_rows * occ_width, piece.shape[2])
    product = jnp.dot(flat, vir_masked, preferred_element_type=jnp.float32)
    return product.reshape(slab_rows, occ_width, -1).astype(jnp.bfloat16)


def solution(mesh):
    placed = (
        P("aux", "ao", None, "orb", None),
        P("ao", None),
        P("ao"),
        P("ao", "orb"),
        P("ao", "orb"),
        P("aux", "ao"),
        P(None, "ao"),
    )
    return jax.shard_map(
        local, mesh=mesh, in_specs=placed, out_specs=P("aux", "orb", "ao"), check_vma=False
    )
```

profile of v0, /device:TPU:1, one launch (start us, length us, event | category | flops | bytes accessed | tf_op | source)
XLA Modules:
  0.0 183.8 jit_solution(8361173918025073191)
XLA Ops:
  6.5 0.0 all-gather.4.cloned.1.call-start
  6.5 0.7 all-gather.4.cloned.1.call-update
  7.3 0.0 all-gather.8.cloned.1.call-start
  7.3 0.8 dynamic-slice_convert_fusion
  8.1 0.1 copy.8
  8.2 0.3 broadcast_in_dim.9
  8.5 1.7 bitcast_multiply_fusion
  10.2 0.0 all-gather.8.cloned.1.call-update
  10.3 0.0 all-gather.6.cloned.1.call-start
  11.6 0.7 fusion.19
  12.3 0.8 broadcast_multiply_fusion
  13.0 22.4 %all_gather.12 = bf16[2048,128]{1,0:T(8,128)(2,1)S(1)} all-gather(bf16[128,128]{1,0:T(8,128)(2,1)S(1)} %broadcast_multiply_fusion), channel_id=1, replica_groups=mesh['aux'=8,'ao'=16,'orb'=4] {'ao'}, dimensions={0}, use_global_device_ids=true | all-gather | bytes 557056 | tf_op jit(solution)/shard_map/all_gather | solution.py:15
  35.4 0.6 gather_fusion
  36.0 14.8 %all-gather.4.cloned.1.call-done = bf16[16,1,4,128,128]{4,3,2,1,0:T(8,128)(2,1)} async-done(((bf16[16,1,4,32,128]{4,3,2,1,0:T(8,128)(2,1)}), bf16[16,1,4,128,128]{4,3,2,1,0:T(8,128)(2,1)}) %all-gather.4.cloned.1.call-update) | async-done | bytes 2097168 | tf_op jit(solution)/shard_map/all_gather | solution.py:16
  50.9 2.9 %fusion.13 = bf16[16,128,128]{2,1,0:T(8,128)(2,1)} fusion(bf16[16,1,4,128,128]{4,3,2,1,0:T(8,128)(2,1)} %all-gather.4.cloned.1.call-done, bf16[4,128,128]{2,1,0:T(8,128)(2,1)S(1)} %gather_fusion, bf16[4]{0:T(256)(128)(2,1)S(1)} %compare_convert_fusion), kind=kOutput, calls=%fused_computation.8 | convolution fusion | flops 268959744 | bytes 2752520 | tf_op jit(solution)/shard_map/kri,pkrv->piv/dot_general | solution.py:26
  53.8 0.0 all-gather.6.cloned.1.call-update
  53.8 39.3 %all-gather.8.cloned.1.call-done = bf16[2048,512]{1,0:T(8,128)(2,1)} async-done(((bf16[256,512]{1,0:T(8,128)(2,1)}), bf16[2048,512]{1,0:T(8,128)(2,1)}) %all-gather.8.cloned.1.call-update) | async-done | bytes 2097168 | tf_op jit(solution)/shard_map/all_gather | solution.py:21
  93.1 74.3 %all-gather.6.cloned.1.call-done = bf16[16,128,2048]{2,1,0:T(8,128)(2,1)} async-done(((bf16[16,128,128]{2,1,0:T(8,128)(2,1)}), bf16[16,128,2048]{2,1,0:T(8,128)(2,1)}) %all-gather.6.cloned.1.call-update) | async-done | bytes 8388624 | tf_op jit(solution)/shard_map/all_gather | solution.py:29
  167.4 9.8 %fusion.4 = bf16[16,128,512]{2,1,0:T(8,128)(2,1)} fusion(bf16[16,128,2048]{2,1,0:T(8,128)(2,1)} %all-gather.6.cloned.1.call-done, bf16[2048,512]{1,0:T(8,128)(2,1)} %all-gather.8.cloned.1.call-done), kind=kOutput, calls=%fused_computation.5 | convolution fusion | flops 4296015872 | bytes 12582912 | tf_op jit(solution)/shard_map/dot_general | solution.py:31
  (3 shorter events, 0.0 us)
Async XLA Ops:
  6.5 44.3 %all-gather.4.cloned.1.call-start = ((), (), s32[]{:S(2)}) async-start(), calls=%async_computation | async-start | bytes 2621440 | tf_op jit(solution)/shard_map/all_gather | solution.py:16
  7.3 85.9 %all-gather.8.cloned.1.call-start = ((), (), s32[]{:S(2)}) async-start(), calls=%async_computation.2 | async-start | bytes 2359296 | tf_op jit(solution)/shard_map/all_gather | solution.py:21
  10.3 157.2 %all-gather.6.cloned.1.call-start = ((), (), s32[]{:S(2)}) async-start(), calls=%async_computation.1 | async-start | bytes 8912896 | tf_op jit(solution)/shard_map/all_gather | solution.py:29
Sparse Core Ops, SparseCore 0:
  9.4 41.3 all-gather.3
  52.9 40.1 all-gather.7
  95.2 72.2 all-gather.5
where the time goes:
time: 184 us
  waiting for transfers between devices  129 us (70%)
  blocking collectives  22.4 us (12%)
  between operations  14.4 us (8%)
  matrix products  12.7 us (7%)
  other arithmetic  3.9 us (2%)
    all_gather x1, waiting for transfers between devices, local(): piece = lax.all_gather(half, 'ao', axis=2, tiled=True)  74.3 us
    all_gather x1, waiting for transfers between devices, local(): vir_masked = lax.all_gather(virtual_coeff * dom, 'aux', axis=0, tiled=True)  39.3 us
    all_gather x1, blocking collectives, local(): all_occ = lax.all_gather(occ_local, 'ao', axis=0, tiled=True)  22.4 us
    all_gather x1, waiting for transfers between devices, local(): all_ints = lax.all_gather(integrals, 'orb', axis=3, tiled=True)  14.8 us
    dot_general x1, matrix products, local(): product = jnp.dot(flat, vir_masked, preferred_element_type=jnp.float32)  9.82 us
  transfers between devices with their start and end apart: 3, of which 3 were waited for; matrix products, arithmetic and copies ran while one was open for 4% of the time, Pallas kernels for 0%

commit v1 on v0

--- a/solution.py
+++ b/solution.py
@@ -18,7 +18,9 @@
     first = lax.axis_index("aux") * vir_blocks
     dom = lax.dynamic_slice_in_dim(virtual_domain, first, vir_blocks, axis=0).astype(jnp.bfloat16)
     dom = jnp.repeat(jnp.repeat(dom, block_size, axis=0), block_size, axis=1)
-    vir_masked = lax.all_gather(virtual_coeff * dom, "aux", axis=0, tiled=True)
+    vir_masked = jnp.concatenate(
+        lax.all_to_all(jnp.stack([virtual_coeff * dom] * lax.axis_size("aux")), "aux", 0, 0), axis=0
+    )
     picked = all_occ.reshape(-1, block_size, occ_width)[partner[0]]
     slots = jnp.arange(slot_count, dtype=jnp.int32)
     live = (slots < pair_count[0]).astype(jnp.bfloat16)

time: 184 us -> 139 us (0.76)
  waiting for transfers between devices: 129 us -> 30.7 us
  blocking collectives: 22.4 us -> 78.9 us
  other arithmetic: 3.9 us -> 1.56 us
    all_gather x1, waiting for transfers between devices: 74.3 us -> 12.1 us  [local(): piece = lax.all_gather(half, 'ao', axis=2, tiled=True)]
    all_to_all x0 -> x1, blocking collectives: none -> 56.5 us  [local(): lax.all_to_all(jnp.stack([virtual_coeff * dom] * lax.axis_size('aux')), '...]
    all_gather x1 -> x0, waiting for transfers between devices: 39.3 us -> none  [local(): vir_masked = lax.all_gather(virtual_coeff * dom, 'aux', axis=0, tiled=True)]
    all_gather x1, waiting for transfers between devices: 14.8 us -> 17.9 us  [local(): all_ints = lax.all_gather(integrals, 'orb', axis=3, tiled=True)]
  transfers between devices with their start and end apart: 3 -> 2, of which waited for: 3 -> 2; matrix products, arithmetic and copies ran while one was open for 4% -> 2% of each run, Pallas kernels for 0% -> 0%
where the time goes in v1:
time: 139 us
  blocking collectives  78.9 us (57%)
  waiting for transfers between devices  30.7 us (22%)
  between operations  14.8 us (11%)
  matrix products  12 us (9%)
  other arithmetic  1.56 us (1%)
    all_to_all x1, blocking collectives, local(): lax.all_to_all(jnp.stack([virtual_coeff * dom] * lax.axis_size('aux')), '...  56.5 us
    all_gather x1, blocking collectives, local(): all_occ = lax.all_gather(occ_local, 'ao', axis=0, tiled=True)  22.4 us
    all_gather x1, waiting for transfers between devices, local(): all_ints = lax.all_gather(integrals, 'orb', axis=3, tiled=True)  17.9 us
    all_gather x1, waiting for transfers between devices, local(): piece = lax.all_gather(half, 'ao', axis=2, tiled=True)  12.1 us
    dot_general x1, matrix products, local(): product = jnp.dot(flat, vir_masked, preferred_element_type=jnp.float32)  9.07 us
    dot_general x1, matrix products, local(): jnp.einsum('kri,pkrv->piv', picked, all_ints[:, 0], preferred_element_typ...  2.94 us
  transfers between devices with their start and end apart: 2, of which 2 were waited for; matrix products, arithmetic and copies ran while one was open for 2% of the time, Pallas kernels for 0%

profile of v1, /device:TPU:1, one launch (start us, length us, event | category | flops | bytes accessed | tf_op | source)
XLA Modules:
  0.0 139.2 jit_solution(8377472458960383007)
XLA Ops:
  6.5 0.0 all-gather.3.cloned.1.call-start
  6.5 0.7 all-gather.3.cloned.1.call-update
  7.3 0.0 all-gather.5.cloned.1.call-start
  8.6 0.7 fusion.14
  9.3 0.0 copy-start.1
  9.3 0.8 broadcast_multiply_fusion
  10.0 22.4 %all_gather.9 = bf16[2048,128]{1,0:T(8,128)(2,1)S(1)} all-gather(bf16[128,128]{1,0:T(8,128)(2,1)S(1)} %broadcast_multiply_fusion), channel_id=1, replica_groups=mesh['aux'=8,'ao'=16,'orb'=4] {'ao'}, dimensions={0}, use_global_device_ids=true | all-gather | bytes 557056 | tf_op jit(solution)/shard_map/all_gather | solution.py:15
  32.4 0.0 copy-start
  32.4 0.6 gather_fusion
  33.0 17.9 %all-gather.3.cloned.1.call-done = bf16[16,1,4,128,128]{4,3,2,1,0:T(8,128)(2,1)} async-done(((bf16[16,1,4,32,128]{4,3,2,1,0:T(8,128)(2,1)}), bf16[16,1,4,128,128]{4,3,2,1,0:T(8,128)(2,1)}) %all-gather.3.cloned.1.call-update) | async-done | bytes 2097168 | tf_op jit(solution)/shard_map/all_gather | solution.py:16
  50.9 2.9 %fusion.8 = bf16[16,128,128]{2,1,0:T(8,128)(2,1)} fusion(bf16[16,1,4,128,128]{4,3,2,1,0:T(8,128)(2,1)} %all-gather.3.cloned.1.call-done, bf16[4,128,128]{2,1,0:T(8,128)(2,1)S(1)} %gather_fusion, bf16[4]{0:T(256)(128)(2,1)S(1)} %compare_convert_fusion), kind=kOutput, calls=%fused_computation.6 | convolution fusion | flops 268959744 | bytes 2752520 | tf_op jit(solution)/shard_map/kri,pkrv->piv/dot_general | solution.py:28
  53.8 0.0 all-gather.5.cloned.1.call-update
  53.8 0.0 copy-done.1
  53.8 0.1 dynamic-slice_convert_fusion
  53.9 0.1 copy.8
  54.0 0.3 broadcast_in_dim.9
  54.4 0.0 copy-done
  54.4 0.2 stack.2
  54.6 56.5 %all_to_all.5 = bf16[8,256,512]{2,1,0:T(8,128)(2,1)S(1)} all-to-all(bf16[8,256,512]{2,1,0:T(8,128)(2,1)S(1)} %stack.2), channel_id=1, replica_groups=mesh['aux'=8,'ao'=16,'orb'=4] {'aux'}, dimensions={0} | all-to-all | bytes 4194304 | tf_op jit(solution)/shard_map/all_to_all | solution.py:22
  111.1 12.1 %all-gather.5.cloned.1.call-done = bf16[16,128,2048]{2,1,0:T(8,128)(2,1)} async-done(((bf16[16,128,128]{2,1,0:T(8,128)(2,1)}), bf16[16,128,2048]{2,1,0:T(8,128)(2,1)}) %all-gather.5.cloned.1.call-update) | async-done | bytes 8388624 | tf_op jit(solution)/shard_map/all_gather | solution.py:31
  123.2 9.1 %convolution_convert_fusion = bf16[16,128,512]{2,1,0:T(8,128)(2,1)} fusion(bf16[16,128,2048]{2,1,0:T(8,128)(2,1)} %all-gather.5.cloned.1.call-done, bf16[2048,512,1]{1,0,2:T(8,128)(2,1)S(1)} %bitcast.38), kind=kOutput, calls=%fused_computation.3 | convolution fusion | flops 4296015872 | bytes 12582912 | tf_op jit(solution)/shard_map/dot_general | solution.py:33
  (4 shorter events, 0.1 us)
Async XLA Ops:
  6.5 44.3 %all-gather.3.cloned.1.call-start = ((), (), s32[]{:S(2)}) async-start(), calls=%async_computation.1 | async-start | bytes 2621440 | tf_op jit(solution)/shard_map/all_gather | solution.py:16
  7.3 116.0 %all-gather.5.cloned.1.call-start = ((), (), s32[]{:S(2)}) async-start(), calls=%async_computation.2 | async-start | bytes 8912896 | tf_op jit(solution)/shard_map/all_gather | solution.py:31
  9.3 44.6 %copy-start.1 = (s32[16,4]{0,1:T(4,128)S(1)}, s32[16,4]{0,1:T(4,128)}, u32[]{:S(2)}) copy-start(s32[16,4]{0,1:T(4,128)} %param.13) | copy-start | bytes 772
  32.4 22.0 %copy-start = (bf16[256,512]{1,0:T(8,128)(2,1)S(1)}, bf16[256,512]{1,0:T(8,128)(2,1)}, u32[]{:S(2)}) copy-start(bf16[256,512]{1,0:T(8,128)(2,1)} %param.12) | copy-start | bytes 786436
Sparse Core Ops, SparseCore 0:
  9.4 41.3 all-gather.2
  53.9 69.2 all-gather.4
